TPU v7x, 32 devices: a whole 2x2x4 slice. The times are simulated.
32 devices in a mesh: sfc: 16 (over z, y, x), lev: 2 (over core).
Axes of the slice: x: 2, y: 2, z: 4, core: 2. Of those that a mesh axis runs over, the one named last changes fastest.
Arguments:
- air_state: float32 [24, 8, 32768], P(None, 'lev', 'sfc'), may hold values from -6 to 6
- metric: float32 [2, 2048], P(None, 'sfc'), may hold values from -5 to 5
- jacobian: float32 [2048], P('sfc'), may hold values from 0.25 to 4
- edge_nbr: int32 [4, 2048], P(None, 'sfc'), may hold values from 0 to 2047, as said below
- edge_side: int32 [4, 2048], P(None, 'sfc'), may hold values from 0 to 3
- coszen: float32 [32768], P('sfc'), may hold values from -1 to 1
- kappa_base: float32 [112], replicated, may hold values from 0.02 to 2
- band_kappa: float32 [112, 20], replicated, may hold values from 0.005 to 0.2
- solar_weight: float32 [112], replicated, may hold values from 0.5 to 2
- stretch_pos: int32 [32768], P('sfc'), may hold values from 0 to 32767, as said below
- stretch_src: int32 [32768], P('sfc'), may hold values from 0 to 32767, as said below
Outputs:
- new_state: float32 [24, 8, 32768], P(None, 'lev', 'sfc')
- surface_flux: float32 [32768], P(('sfc', 'lev'))
Inputs may be any that keep to these rules, and one draw needn't show every extreme that they name: edge_nbr[k, g] lies within 128 elements of g along the curve, cyclically over 2048 elements; that distance is reached. stretch_pos is a permutation of the columns and stretch_src its inverse; column c belongs to the stretch of device stretch_pos[c] // 2048; each device receives 2048 columns, at most 256 of them from one device, a bound reached in every draw; the columns that one device sends to one device take consecutive stretch positions. `stretch_src`: the inverse of stretch_pos.
All inputs are finite; a program needn't handle non-finite values.
Results may differ from a plain program's by a relative error of at most 0.0001.
Values sent between devices are 32-bit elements; how exact they have to be, the bound alone decides.
A program may use at most 64 MiB of HBM per device.

v0:
```python
import functools

import jax
import jax.numpy as jnp
import numpy as np
from jax import lax
from jax.experimental import pallas as pl
from jax.experimental.pallas import tpu as pltpu
from jax.sharding import PartitionSpec as P

NODES = 16
GLL_POINTS = np.array([-1.0, -1.0 / np.sqrt(5.0), 1.0 / np.sqrt(5.0), 1.0])
EDGE_NODES = ((4, 8), (13, 14), (11, 7), (2, 1))
STEP_DYN = 0.2
DEPTH_UNIT = 0.05
HEAT_SCALE = 0.1
FLUX_SCALE = 0.02
F32 = jnp.float32
BF16 = jnp.bfloat16


def derivative_matrix():
    spacing = GLL_POINTS[:, None] - GLL_POINTS[None, :]
    unit_diag = np.eye(4)
    safe_space = np.where(unit_diag > 0, 1.0, spacing)
    weights_row = np.prod(safe_space, axis=1)
    derivative = weights_row[:, None] / weights_row[None, :] / safe_space
    inverse_gap = np.where(unit_diag > 0, 0.0, 1.0 / safe_space)
    return np.where(unit_diag > 0, inverse_gap.sum(axis=1)[:, None], derivative)


def split2(x):
    high = x.astype(BF16)
    return high, (x - high.astype(F32)).astype(BF16)


def dot(a, b):
    return jnp.dot(a, b, preferred_element_type=F32)


MESH = pl.DeviceIdType.MESH
EDGES = tuple(n for pair in EDGE_NODES for n in pair)
INNER = tuple(n for n in range(NODES) if n not in EDGES)


def column(row):
    n = row.shape[1]
    same = lax.broadcasted_iota(jnp.int32, (n, n), 0) == lax.broadcasted_iota(
        jnp.int32, (n, n), 1
    )
    return jnp.sum(jnp.where(same, jnp.broadcast_to(row, (n, n)), 0.0), axis=1, keepdims=True)


def spread_rates(bands, fields):
    tracers = bands.shape[0]
    high, low = split2(-DEPTH_UNIT * bands)
    shape = (tracers, 3 * fields)
    first = lax.broadcasted_iota(jnp.int32, shape, 0) + (fields - tracers)
    lane = lax.broadcasted_iota(jnp.int32, shape, 1)
    pick_high = (lane == first) | (lane == first + fields)
    pick_low = lane == first + 2 * fields
    one = lambda m: jnp.where(m, 1.0, 0.0).astype(BF16)
    mix = lambda a, b: lax.dot_general(a, b, (((0,), (0,)), ((), ())), preferred_element_type=F32)
    return (mix(high, one(pick_high)) + mix(low, one(pick_low))).astype(BF16)


def step_kernel(
    count,
    levels,
    state_ref,
    metric_ref,
    jac_ref,
    nbr_ref,
    side_ref,
    sun_ref,
    base_ref,
    band_ref,
    weight_ref,
    src_ref,
    new_ref,
    flux_ref,
    x_ref,
    out_ref,
    adv,
    edges,
    direct_buf,
    relay_buf,
    sq,
    other_sq,
    flux,
    table,
    edge_send,
    edge_recv,
    swap_send,
    swap_recv,
    flux_send,
    flux_recv,
    in_sem,
    out_sem,
):
    rows, cols = x_ref.shape
    ne = cols // NODES
    fields = rows // levels
    width = 4 * ne
    me, lev = lax.axis_index("sfc"), lax.axis_index("lev")
    odd = lax.rem(me, 2)
    partner = me + 1 - 2 * odd
    onward = lax.rem(me + count + 2 - 4 * odd, count)

    def fetch(l):
        return pltpu.make_async_copy(
            state_ref.at[:, l, :], x_ref.at[l * fields : (l + 1) * fields], in_sem.at[l]
        )

    def store(l):
        return pltpu.make_async_copy(
            out_ref.at[l * fields : (l + 1) * fields], new_ref.at[:, l, :], out_sem.at[l]
        )

    for l in range(levels):
        fetch(l).start()
    barrier = pltpu.get_barrier_semaphore()

    def greet(step, carry):
        pl.semaphore_signal(
            barrier, inc=1, device_id=(lax.rem(me + step, count), lev), device_id_type=MESH
        )
        return carry

    lax.fori_loop(1, count, greet, 0)
    pl.semaphore_signal(barrier, inc=1, device_id=(me, 1 - lev), device_id_type=MESH)

    d = derivative_matrix()
    m0 = jnp.broadcast_to(STEP_DYN * metric_ref[0:1, :], (8, ne))
    m1 = jnp.broadcast_to(STEP_DYN * metric_ref[1:2, :], (8, ne))
    for k in range(4):
        edges[:8, k * ne : (k + 1) * ne] = jnp.broadcast_to(jac_ref[...], (8, ne))

    def chunk(l):
        return slice(0 if l == 0 else 8 + 2 * fields * l, 8 + 2 * fields * (l + 1))

    def direct(l):
        return pltpu.make_async_remote_copy(
            edges.at[chunk(l)],
            direct_buf.at[chunk(l)],
            edge_send.at[0, l],
            edge_recv.at[0, l],
            device_id=(partner, lev),
            device_id_type=MESH,
        )

    def relay(l):
        return pltpu.make_async_remote_copy(
            direct_buf.at[chunk(l)],
            relay_buf.at[chunk(l)],
            edge_send.at[1, l],
            edge_recv.at[1, l],
            device_id=(onward, lev),
            device_id_type=MESH,
        )

    for l in range(levels):

        def advance(r, carry, l=l):
            sl = pl.ds(pl.multiple_of(l * fields + r * 8, 8), 8)
            x = [x_ref[sl, n * ne : (n + 1) * ne] for n in range(NODES)]
            out = []
            for i in range(4):
                for j in range(4):
                    one = sum(float(d[i, a]) * x[4 * a + j] for a in range(4))
                    two = sum(float(d[j, a]) * x[4 * i + a] for a in range(4))
                    out.append(x[4 * i + j] + (m0 * one + m1 * two))
            for n in INNER:
                adv[sl, n * ne : (n + 1) * ne] = out[n]
            start = 8 + 2 * fields * l + r * 8
            seconds = pl.ds(pl.multiple_of(start, 8), 8)
            firsts = pl.ds(pl.multiple_of(start + fields, 8), 8)
            for k, (a, b) in enumerate(EDGE_NODES):
                edges[seconds, k * ne : (k + 1) * ne] = out[b]
                edges[firsts, k * ne : (k + 1) * ne] = out[a]
            return carry

        fetch(l).wait()
        lax.fori_loop(0, fields // 8, advance, 0)
        if l == 0:
            pl.semaphore_wait(barrier, count)
        direct(l).start()

    def swap(half):
        return pltpu.make_async_remote_copy(
            sq.at[half],
            other_sq.at[half],
            swap_send.at[half],
            swap_recv.at[half],
            device_id=(me, 1 - lev),
            device_id_type=MESH,
        )

    def put_squares(half, slot, piece):
        squares = piece * piece
        sq[half, :, slot * ne : (slot + 1) * ne] = sum(
            squares[l * fields : (l + 1) * fields] for l in range(levels)
        )

    for slot, n in enumerate(INNER):
        put_squares(0, slot, adv[:, n * ne : (n + 1) * ne])
    inner_swap = swap(0)
    inner_swap.start()

    top = jnp.where(lev == 0, 1.0, 0.0).astype(F32)
    rates = spread_rates(band_ref[...], fields)
    base = -DEPTH_UNIT * column(base_ref[...])
    weight = column(weight_ref[...])
    whole_light = jnp.sum(weight)

    total_nodes = count * ne
    near = nbr_ref[...] - (me - 1) * ne
    near = jnp.where(near < 0, near + total_nodes, near)
    near = jnp.where(near >= total_nodes, near - total_nodes, near)
    window = jnp.where(near >= ne, 1, 0) + jnp.where(near >= 2 * ne, 1, 0)
    spot = window * (width - ne) + side_ref[...] * ne + near
    target = jnp.concatenate([spot[k : k + 1, :] for k in range(4)], axis=1)

    def choice(w):
        lanes = lax.broadcasted_iota(jnp.int32, (width, width), 0) + w * width
        return jnp.where(lanes == target, 1.0, 0.0).astype(BF16)

    def gather(ref, onehot, l):
        high, low = split2(ref[chunk(l)])
        return dot(high, onehot) + dot(low, onehot)

    def depth_of(sums):
        high = sums.astype(BF16).astype(F32)
        stacked = jnp.concatenate([high, sums - high, high], axis=0).astype(BF16)
        return dot(rates, stacked)

    def light(depth, times):
        return jnp.sum(weight * jnp.exp(depth + times * base), axis=0, keepdims=True)

    join = lambda parts: jnp.concatenate(parts, axis=1)

    def own_depths(pieces):
        running, depths = 0.0, []
        for l in range(levels):
            part = join([p[l * fields : (l + 1) * fields, :] for p in pieces])
            running = running + part * part
            depths.append(depth_of(running))
        return depths

    def radiate(half, slots, nodes, pieces, depths):
        lanes = slice(slots[0] * ne, (slots[-1] + 1) * ne)
        sun = jnp.maximum(join([sun_ref[:, n * ne : (n + 1) * ne] for n in nodes]), 0.0)
        other = depth_of(other_sq[half, :, lanes])
        extra = light(other + top * depths[-1], levels * (1.0 + top))
        above = top * whole_light + (1.0 - top) * extra
        other = (1.0 - top) * other
        for l in range(levels):
            below = light(other + depths[l], (1.0 - top) * levels + (l + 1.0))
            heat = HEAT_SCALE * sun * (above - below)
            row = l * fields + 2
            for s, n in enumerate(nodes):
                out_ref[row : row + 1, n * ne : (n + 1) * ne] = (
                    pieces[s][row : row + 1, :] + heat[:, s * ne : (s + 1) * ne]
                )
            above = below
        ground = FLUX_SCALE * sun * (top * extra + (1.0 - top) * above)
        for s, n in enumerate(nodes):
            flux[n : n + 1, :] = ground[:, s * ne : (s + 1) * ne]

    def forward(l):
        direct(l).wait_recv()
        relay(l).start()

    own_choice = choice(1)
    acc = [gather(edges, own_choice, l) for l in range(levels)]
    forward(0)
    inner_swap.wait()
    for part in range(2):
        slots = range(part * 4, part * 4 + 4)
        nodes = [INNER[s] for s in slots]
        pieces = [adv[:, n * ne : (n + 1) * ne] for n in nodes]
        for n, piece in zip(nodes, pieces):
            out_ref[:, n * ne : (n + 1) * ne] = piece
        radiate(0, slots, nodes, pieces, own_depths(pieces))
        if part == 0:
            forward(1)

    direct_choice, relay_choice = choice(2 - 2 * odd), choice(2 * odd)
    for l in range(levels):
        if l > 1:
            forward(l)
        acc[l] = acc[l] + gather(direct_buf, direct_choice, l)

    firsts = [a for a, _ in EDGE_NODES]
    seconds = [b for _, b in EDGE_NODES]
    sums = [0.0, 0.0]
    for l in range(levels):
        relay(l).wait_recv()
        far = acc[l] + gather(relay_buf, relay_choice, l)
        if l == 0:
            own_jac = jnp.concatenate([jac_ref[...]] * 4, axis=1)
            far_jac = far[0:1, :]
            far = far[8:]
            total = own_jac + far_jac
            own_part, far_part = own_jac / total, far_jac / total
        start = 8 + 2 * fields * l
        own_second = edges[start : start + fields, :]
        own_first = edges[start + fields : start + 2 * fields, :]
        both = (
            (own_part * own_first + far_part * far[:fields], firsts),
            (own_part * own_second + far_part * far[fields:], seconds),
        )
        for p, (values, nodes) in enumerate(both):
            sums[p] = sums[p] + values * values
            for k, n in enumerate(nodes):
                out_ref[l * fields : (l + 1) * fields, n * ne : (n + 1) * ne] = values[
                    :, k * ne : (k + 1) * ne
                ]
    sq[1, :, :width] = sums[0]
    sq[1, :, width:] = sums[1]
    edge_swap = swap(1)
    edge_swap.start()
    ready = []
    for nodes in (firsts, seconds):
        pieces = [out_ref[:, n * ne : (n + 1) * ne] for n in nodes]
        ready.append((nodes, pieces, own_depths(pieces)))
    edge_swap.wait()
    for part, work in enumerate(ready):
        radiate(1, range(part * 4, part * 4 + 4), *work)

    def send(step):
        return pltpu.make_async_remote_copy(
            flux,
            table.at[me],
            flux_send.at[step],
            flux_recv.at[me],
            device_id=(lax.rem(me + step, count), lev),
            device_id_type=MESH,
        )

    def arrive(step):
        peer = lax.rem(me + step, count)
        return pltpu.make_async_remote_copy(
            flux,
            table.at[peer],
            flux_send.at[step],
            flux_recv.at[peer],
            device_id=(peer, lev),
            device_id_type=MESH,
        )

    def start_send(step, carry):
        send(step).start()
        return carry

    def finish(step, carry):
        send(step).wait_send()
        arrive(step).wait_recv()
        return carry

    lax.fori_loop(1, count, start_send, 0)
    for l in range(levels):
        store(l).start()
    table[me] = flux[...]
    taken = flux_ref.shape[1]
    index = src_ref[:, pl.ds(pl.multiple_of(lev * taken, 128), taken)]
    high_index, lane_index = index >> 7, index & 127
    lines = count * cols // 128
    onehot = jnp.where(
        lax.broadcasted_iota(jnp.int32, (lines, taken), 0) == high_index, 1.0, 0.0
    ).astype(BF16)
    mask = lax.broadcasted_iota(jnp.int32, (128, taken), 0) == lane_index
    lax.fori_loop(1, count, finish, 0)
    for l in range(levels):
        store(l).wait()
        direct(l).wait_send()
        relay(l).wait_send()
    values = table[...].reshape(lines, 128).T
    high, _ = split2(values)
    low, tail = split2(values - high.astype(F32))
    picked = dot(high, onehot) + dot(low, onehot) + dot(tail, onehot)
    flux_ref[...] = jnp.sum(jnp.where(mask, picked, 0.0), axis=0, keepdims=True)


def local(
    air_state,
    metric,
    jacobian,
    edge_nbr,
    edge_side,
    coszen,
    kappa_base,
    band_kappa,
    solar_weight,
    stretch_pos,
    stretch_src,
):
    fields, levels, cols = air_state.shape
    ne = cols // NODES
    rows = fields * levels
    count = lax.axis_size("sfc")
    part = cols // lax.axis_size("lev")
    anywhere = pl.BlockSpec(memory_space=pl.ANY)
    vmem = pl.BlockSpec(memory_space=pltpu.VMEM)
    new, flux = pl.pallas_call(
        functools.partial(step_kernel, count, levels),
        in_specs=[anywhere] + [vmem] * 9,
        out_specs=(anywhere, vmem),
        out_shape=(
            jax.ShapeDtypeStruct(air_state.shape, F32),
            jax.ShapeDtypeStruct((1, part), F32),
        ),
        scratch_shapes=[
            pltpu.VMEM((rows, cols), F32),
            pltpu.VMEM((rows, cols), F32),
            pltpu.VMEM((rows, cols), F32),
            pltpu.VMEM((2 * rows + 8, 4 * ne), F32),
            pltpu.VMEM((2 * rows + 8, 4 * ne), F32),
            pltpu.VMEM((2 * rows + 8, 4 * ne), F32),
            pltpu.VMEM((2, fields, cols // 2), F32),
            pltpu.VMEM((2, fields, cols // 2), F32),
            pltpu.VMEM((NODES, ne), F32),
            pltpu.VMEM((count, NODES, ne), F32),
            pltpu.SemaphoreType.DMA((2, levels)),
            pltpu.SemaphoreType.DMA((2, levels)),
            pltpu.SemaphoreType.DMA((2,)),
            pltpu.SemaphoreType.DMA((2,)),
            pltpu.SemaphoreType.DMA((count,)),
            pltpu.SemaphoreType.DMA((count,)),
            pltpu.SemaphoreType.DMA((levels,)),
            pltpu.SemaphoreType.DMA((levels,)),
        ],
        compiler_params=pltpu.CompilerParams(collective_id=0, has_side_effects=True),
        name="step",
    )(
        air_state,
        metric,
        jacobian[None, :],
        edge_nbr,
        edge_side,
        coszen[None, :],
        kappa_base[None, :],
        band_kappa.T,
        solar_weight[None, :],
        stretch_src[None, :],
    )
    return (new, flux.reshape(part))


def solution(mesh):
    return jax.shard_map(
        local,
        mesh=mesh,
        in_specs=(
            P(None, "lev", "sfc"),
            P(None, "sfc"),
            P("sfc"),
            P(None, "sfc"),
            P(None, "sfc"),
            P("sfc"),
            P(),
            P(),
            P(),
            P("sfc"),
            P("sfc"),
        ),
        out_specs=(P(None, "lev", "sfc"), P(("sfc", "lev"))),
        check_vma=False,
    )
```

profile of v0, /device:TPU:0, one launch (start us, length us, event | category | flops | bytes accessed | tf_op | source)
XLA Modules:
  0.0 34.9 jit_solution(4974934477102597077)
XLA Ops:
  0.6 31.5 %step.1 = (f32[24,4,2048]{2,1,0:T(4,128)}, f32[1,1024]{1,0:T(1,128)}) custom-call(f32[24,4,2048]{2,1,0:T(4,128)} %state_ref.1, f32[2,128]{1,0:T(2,128)} %metric_ref.1, f32[1,128]{1,0:T(1,128)} %bitcast.11, s32[4,128]{1,0:T(4,128)} %nbr_ref.1, s32[4,128]{1,0:T(4,128)} %side_ref.1, f32[1,2048]{1,0:T(1,128)} %bitcast.8, f32[1,112]{1,0:T(1,128)} %bitcast.12, ...), custom_call_target="tpu_custom_call" | custom-call | tf_op jit(solution)/shard_map/step/pallas_call | solution.py:405
  32.2 0.0 copy-start
  32.2 2.1 %copy.14 = f32[24,4,2048]{2,1,0:T(4,128)} copy(f32[24,4,2048]{2,1,0:T(4,128)} %get-tuple-element.8) | data formatting | bytes 1572864
  34.3 0.0 copy-done
  34.3 0.6 %copy.15 = f32[1024]{0:T(1024)} copy(f32[1024]{0:T(1024)S(1)} %bitcast.10) | data formatting | bytes 8192
Async XLA Ops:
  32.2 2.1 %copy-start = (f32[1,1024]{1,0:T(1,128)S(1)}, f32[1,1024]{1,0:T(1,128)}, u32[]{:S(2)}) copy-start(f32[1,1024]{1,0:T(1,128)} %get-tuple-element.5) | copy-start | bytes 12292
where the time goes:
time: 35.1 us; the launch traced here: 34.9 us
  Pallas kernels  31.5 us (90%)
  local copies, waits for them, and re-layouts  2.69 us (8%)
  between operations  0.65 us (2%)
    pallas_call x1, Pallas kernels, local(): pl.pallas_call(functools.partial(step_kernel, count, levels), in_specs=[a...  31.5 us
    unnamed x4, local copies, waits for them, and re-layouts  2.69 us

commit v1 on v0

v1 whole, which is shorter than its diff:
```python
import functools

import jax
import jax.numpy as jnp
import numpy as np
from jax import lax
from jax.experimental import pallas as pl
from jax.experimental.pallas import tpu as pltpu
from jax.sharding import PartitionSpec as P

NODES = 16
GLL_POINTS = np.array([-1.0, -1.0 / np.sqrt(5.0), 1.0 / np.sqrt(5.0), 1.0])
EDGE_NODES = ((4, 8), (13, 14), (11, 7), (2, 1))
STEP_DYN = 0.2
DEPTH_UNIT = 0.05
HEAT_SCALE = 0.1
FLUX_SCALE = 0.02
F32 = jnp.float32
BF16 = jnp.bfloat16


def derivative_matrix():
    spacing = GLL_POINTS[:, None] - GLL_POINTS[None, :]
    unit_diag = np.eye(4)
    safe_space = np.where(unit_diag > 0, 1.0, spacing)
    weights_row = np.prod(safe_space, axis=1)
    derivative = weights_row[:, None] / weights_row[None, :] / safe_space
    inverse_gap = np.where(unit_diag > 0, 0.0, 1.0 / safe_space)
    return np.where(unit_diag > 0, inverse_gap.sum(axis=1)[:, None], derivative)


def split2(x):
    high = x.astype(BF16)
    return high, (x - high.astype(F32)).astype(BF16)


def dot(a, b):
    return jnp.dot(a, b, preferred_element_type=F32)


MESH = pl.DeviceIdType.MESH
EDGES = tuple(n for pair in EDGE_NODES for n in pair)
INNER = tuple(n for n in range(NODES) if n not in EDGES)


def column(row):
    n = row.shape[1]
    same = lax.broadcasted_iota(jnp.int32, (n, n), 0) == lax.broadcasted_iota(
        jnp.int32, (n, n), 1
    )
    return jnp.sum(jnp.where(same, jnp.broadcast_to(row, (n, n)), 0.0), axis=1, keepdims=True)


def log2(n):
    assert n & (n - 1) == 0
    return n.bit_length() - 1


def mix(a, b):
    return lax.dot_general(a, b, (((0,), (0,)), ((), ())), preferred_element_type=F32)


def spread_rates(bands, rows, per):
    high, low = split2(-DEPTH_UNIT * bands)
    shape = (bands.shape[0], 3 * rows)
    tracer = lax.broadcasted_iota(jnp.int32, shape, 0)
    lane = lax.broadcasted_iota(jnp.int32, shape, 1)
    third = jnp.where(lane >= rows, 1, 0) + jnp.where(lane >= 2 * rows, 1, 0)
    hit = (lane - third * rows) >> log2(per) == tracer
    one = lambda m: jnp.where(m, 1.0, 0.0).astype(BF16)
    return mix(high, one(hit & (third < 2))) + mix(low, one(hit & (third == 2)))


def stack3(x):
    high = x.astype(BF16).astype(F32)
    return jnp.concatenate([high, x - high, high], axis=0).astype(BF16)


def step_kernel(
    count,
    levels,
    chunks,
    state_ref,
    metric_hbm,
    jac_hbm,
    nbr_hbm,
    side_hbm,
    sun_hbm,
    base_hbm,
    band_hbm,
    weight_hbm,
    src_hbm,
    pos_hbm,
    new_ref,
    table_ref,
    index_ref,
    x_ref,
    seconds,
    firsts,
    direct_buf,
    relay_buf,
    cross_buf,
    mixed,
    mixed_buf,
    far0,
    far1,
    merged,
    choices,
    glow,
    heats,
    sq_inner,
    other_inner,
    sq_edge,
    other_edge,
    metric_ref,
    jac_ref,
    nbr_ref,
    side_ref,
    sun_ref,
    base_ref,
    band_ref,
    weight_ref,
    src_ref,
    pos_ref,
    their_nbr,
    their_side,
    direct_jac,
    relay_jac,
    spots,
    outbox,
    inbox,
    edge_send,
    edge_recv,
    meta_send,
    meta_recv,
    swap_send,
    swap_recv,
    flux_send,
    flux_recv,
    in_sem,
    small_sem,
):
    rows, cols = x_ref.shape
    ne = cols // NODES
    fields = rows // levels
    tracers = band_ref.shape[0]
    skip = rows - tracers * levels
    width = 4 * ne
    me, lev = lax.axis_index("sfc"), lax.axis_index("lev")
    odd = lax.rem(me, 2)
    partner = me + 1 - 2 * odd
    onward = lax.rem(me + count + 2 - 4 * odd, count)
    backward = lax.rem(me + count - 2 + 4 * odd, count)
    barrier = pltpu.get_barrier_semaphore()

    def greet(step, carry):
        pl.semaphore_signal(
            barrier, inc=1, device_id=(lax.rem(me + step, count), lev), device_id_type=MESH
        )
        return carry

    lax.fori_loop(1, count, greet, 0)
    pl.semaphore_signal(barrier, inc=1, device_id=(me, 1 - lev), device_id_type=MESH)

    small = [
        pltpu.make_async_copy(a, b, small_sem.at[i])
        for i, (a, b) in enumerate(
            (
                (metric_hbm, metric_ref),
                (jac_hbm, jac_ref),
                (nbr_hbm, nbr_ref),
                (side_hbm, side_ref),
                (band_hbm, band_ref),
                (base_hbm, base_ref),
                (weight_hbm, weight_ref),
                (sun_hbm, sun_ref),
                (pos_hbm, pos_ref),
                (src_hbm, src_ref),
            )
        )
    ]

    def fetch(f):
        return pltpu.make_async_copy(
            state_ref.at[f], x_ref.at[f * levels : (f + 1) * levels], in_sem.at[f]
        )

    for copy in small[:2]:
        copy.start()
    for start, stop in chunks:
        for f in range(start // levels, stop // levels):
            fetch(f).start()
        if start == chunks[0][0]:
            for copy in small[2:]:
                copy.start()

    d = derivative_matrix()

    def remote(src, dst, send, recv, to):
        return pltpu.make_async_remote_copy(
            src, dst, send, recv, device_id=to, device_id_type=MESH
        )

    def edge_copy(kind, src, dst, to):
        def make(c):
            part = slice(*chunks[c])
            return remote(
                src.at[part], dst.at[part], edge_send.at[kind, c], edge_recv.at[kind, c], (to, lev)
            )

        return make

    direct = edge_copy(0, seconds, direct_buf, partner)
    relay = edge_copy(1, direct_buf, relay_buf, onward)
    cross = edge_copy(2, firsts, cross_buf, backward)
    blend = edge_copy(3, mixed, mixed_buf, partner)
    meta = [
        remote(a, b, meta_send.at[i], meta_recv.at[i], (to, lev))
        for i, (a, b, to) in enumerate(
            (
                (jac_ref, direct_jac, partner),
                (direct_jac, relay_jac, onward),
                (nbr_hbm, their_nbr, partner),
                (side_hbm, their_side, partner),
            )
        )
    ]

    small[0].wait()
    small[1].wait()
    m0 = jnp.broadcast_to(STEP_DYN * metric_ref[0:1, :], (8, ne))
    m1 = jnp.broadcast_to(STEP_DYN * metric_ref[1:2, :], (8, ne))

    def advance(r, carry):
        sl = pl.ds(pl.multiple_of(r * 8, 8), 8)
        x = [x_ref[sl, n * ne : (n + 1) * ne] for n in range(NODES)]
        out = []
        for i in range(4):
            for j in range(4):
                one = sum(float(d[i, a]) * x[4 * a + j] for a in range(4))
                two = sum(float(d[j, a]) * x[4 * i + a] for a in range(4))
                out.append(x[4 * i + j] + (m0 * one + m1 * two))
        for n in INNER:
            new_ref[sl, n * ne : (n + 1) * ne] = out[n]
        for k, (a, b) in enumerate(EDGE_NODES):
            seconds[sl, k * ne : (k + 1) * ne] = out[b]
            firsts[sl, k * ne : (k + 1) * ne] = out[a]
        return carry

    last = len(chunks) - 1
    for c, (start, stop) in enumerate(chunks):
        for f in range(start // levels, stop // levels):
            fetch(f).wait()
        lax.fori_loop(start // 8, stop // 8, advance, 0)
        if c == 0:
            pl.semaphore_wait(barrier, count)
            for i in (0, 2, 3):
                meta[i].start()
        direct(c).start()
        if c < last:
            cross(c).start()

    def swap(part, a, b):
        return remote(a, b, swap_send.at[part], swap_recv.at[part], (me, 1 - lev))

    thick = tracers * levels
    padded = other_inner.shape[0]
    row = lax.broadcasted_iota(jnp.int32, (padded, 3 * thick), 0)
    lane = lax.broadcasted_iota(jnp.int32, (padded, 3 * thick), 1)
    lane = jnp.where(lane >= thick, lane - thick, lane)
    level_sum = jnp.where(lane >> log2(levels) == row, 1.0, 0.0).astype(BF16)

    def inner_tracers(part):
        nodes = INNER[part * 4 : part * 4 + 4]
        return jnp.concatenate(
            [new_ref[skip:, n * ne : (n + 1) * ne] for n in nodes], axis=1
        )

    for part in range(2):
        values = inner_tracers(part)
        sq_inner[:, part * width : (part + 1) * width] = dot(
            level_sum, stack3(values * values)
        )
    inner_swap = swap(0, sq_inner, other_inner)
    inner_swap.start()
    edge_swaps = [swap(1 + p, sq_edge.at[p], other_edge.at[p]) for p in range(2)]

    for copy in small[2:]:
        copy.wait()
    top = jnp.where(lev == 0, 1.0, 0.0).astype(F32)
    rates = spread_rates(band_ref[...], thick, levels)
    own_level = lax.rem(lax.broadcasted_iota(jnp.int32, rates.shape, 1), levels)
    own_rates = [jnp.where(own_level <= l, rates, 0.0).astype(BF16) for l in range(levels)]
    sum_rates = spread_rates(band_ref[...], padded, 1).astype(BF16)
    base = -DEPTH_UNIT * column(base_ref[...])
    weight = column(weight_ref[...])

    total_nodes = count * ne

    def spot_of(nbr, side, where):
        near = nbr - (where - 1) * ne
        near = jnp.where(near < 0, near + total_nodes, near)
        near = jnp.where(near >= total_nodes, near - total_nodes, near)
        window = jnp.where(near >= ne, 1, 0) + jnp.where(near >= 2 * ne, 1, 0)
        spot = window * (width - ne) + side * ne + near
        return jnp.concatenate([spot[k : k + 1, :] for k in range(4)], axis=1)

    def choose(i, target, w):
        lanes = lax.broadcasted_iota(jnp.int32, (width, width), 0) + w * width
        choices[i] = jnp.where(lanes == target, 1.0, 0.0).astype(BF16)

    def pick(values, i):
        n = values.shape[0]
        high, low = split2(values)
        both = dot(jnp.concatenate([high, low], axis=0), choices[i])
        return both[:n] + both[n:]

    def pick_jac(ref, i):
        wide = jnp.concatenate([jnp.broadcast_to(ref[...], (16, ne))] * 4, axis=1)
        return pick(wide, i)[0:1]

    def own_glow(slot, stacked):
        for l in range(levels):
            depth = dot(own_rates[l], stacked) + (l + 1.0) * base
            glow[slot, l] = weight * jnp.exp(depth)

    def finish(slot, other, sun):
        far = jnp.exp(dot(sum_rates, stack3(other)) + levels * base)
        keep = top + (1.0 - top) * far
        total = lambda v: jnp.sum(v, axis=0, keepdims=True)
        above = total(weight * keep)
        heat = []
        for l in range(levels):
            below = total(glow[slot, l] * keep)
            heat.append(HEAT_SCALE * sun * (above - below))
            above = below
        ground = FLUX_SCALE * sun * total(glow[slot, levels - 1] * far)
        return jnp.concatenate(heat, axis=0), ground

    def join(ref, row, nodes):
        return jnp.concatenate(
            [ref[row : row + 1, n * ne : (n + 1) * ne] for n in nodes], axis=1
        )

    lines = table_ref.shape[0]
    per = lines // count
    shift = log2(cols)

    def runs(device, place):
        ids = lax.broadcasted_iota(jnp.int32, (count, cols), 0)
        match = ids == device
        place = place.astype(F32)
        least = jnp.min(jnp.where(match, place, 1e9), axis=1, keepdims=True)
        return (place - jnp.sum(jnp.where(match, least, 0.0), axis=0, keepdims=True)).astype(
            jnp.int32
        )

    goes = pos_ref[...] >> shift
    rank = runs(goes, pos_ref[...])
    spots[0:1, :] = goes * per + (rank >> 7)
    spots[1:2, :] = rank & 127
    comes = src_ref[...] >> shift
    rank = runs(comes, lax.broadcasted_iota(jnp.int32, (1, cols), 1))
    spots[2:3, :] = comes * (per * 128) + rank
    taken = index_ref.shape[1]
    index_ref[...] = spots[2:3, pl.ds(pl.multiple_of(lev * taken, 128), taken)]

    def scatter(ground, nodes):
        line, lane = join(spots, 0, nodes), join(spots, 1, nodes)
        n = line.shape[1]
        there = lax.broadcasted_iota(jnp.int32, (lines, n), 0) == line
        high, _ = split2(ground)
        low, tail = split2(ground - high.astype(F32))
        parts = [jnp.where(there, v.astype(F32), 0.0) for v in (high, low, tail)]
        onehot = jnp.where(
            lax.broadcasted_iota(jnp.int32, (128, n), 0) == lane, 1.0, 0.0
        ).astype(BF16)
        out = lax.dot_general(
            jnp.concatenate(parts, axis=0).astype(BF16),
            onehot,
            (((1,), (1,)), ((), ())),
            preferred_element_type=F32,
        )
        return out[:lines] + out[lines : 2 * lines] + out[2 * lines :]

    def inner_part(part):
        nodes = INNER[part * 4 : part * 4 + 4]
        values = inner_tracers(part)
        own_glow(part, stack3(values * values))
        other = other_inner[:, part * width : (part + 1) * width]
        heat, ground = finish(part, other, jnp.maximum(join(sun_ref, 0, nodes), 0.0))
        for s, n in enumerate(nodes):
            lanes = slice(n * ne, (n + 1) * ne)
            new_ref[2 * levels : 3 * levels, lanes] = (
                new_ref[2 * levels : 3 * levels, lanes] + heat[:, s * ne : (s + 1) * ne]
            )
        return scatter(ground, nodes)

    target = spot_of(nbr_ref[...], side_ref[...], me)
    choose(0, target, 1)
    far1[...] = pick(firsts[...], 0)
    far0[...] = pick(seconds[...], 0)
    own_jac = pick_jac(jac_ref, 0)
    inner_swap.wait_recv()
    table = inner_part(0)

    def forward(c):
        direct(c).wait_recv()
        relay(c).start()

    meta[0].wait_recv()
    meta[1].start()
    forward(0)
    forward(1)
    meta[2].wait_recv()
    meta[3].wait_recv()
    theirs = spot_of(their_nbr[...], their_side[...], partner)
    choose(1, theirs, 2 * odd)
    choose(2, theirs, 2 - 2 * odd)
    mixed[...] = pick(firsts[...], 1)

    def answer(c):
        part = slice(*chunks[c])
        cross(c).wait_recv()
        mixed[part] = mixed[part] + pick(cross_buf[part], 2)
        blend(c).start()

    for c in range(last):
        answer(c)
        if 2 + c < last:
            forward(2 + c)
    cross(last).start()
    forward(last)
    table = table + inner_part(1)

    choose(3, target, 2 - 2 * odd)
    choose(4, target, 2 * odd)
    for c in range(last):
        part = slice(*chunks[c])
        far0[part] = far0[part] + pick(direct_buf[part], 3)
    meta[1].wait_recv()
    far_jac = own_jac + pick_jac(direct_jac, 3) + pick_jac(relay_jac, 4)
    mine = jnp.concatenate([jac_ref[...]] * 4, axis=1)
    own_part, far_part = mine / (mine + far_jac), far_jac / (mine + far_jac)
    nodes_of = [[a for a, _ in EDGE_NODES], [b for _, b in EDGE_NODES]]

    def put(p, part, values):
        for k, n in enumerate(nodes_of[p]):
            new_ref[part, n * ne : (n + 1) * ne] = values[:, k * ne : (k + 1) * ne]

    def merge(p, c):
        part = slice(*chunks[c])
        if p == 0:
            relay(c).wait_recv()
            far, own = far0[part] + pick(relay_buf[part], 4), firsts[part]
        else:
            blend(c).wait_recv()
            far, own = far1[part] + mixed_buf[part], seconds[part]
        return own_part * own + far_part * far

    def settle(p, c):
        part = slice(*chunks[c])
        values = merge(p, c)
        merged[p, part] = values
        put(p, part, values)

    def share(p):
        values = merged[p, skip:]
        stacked = stack3(values * values)
        sq_edge[p] = dot(level_sum, stacked)
        edge_swaps[p].start()
        own_glow(p, stacked)

    def shine(p):
        edge_swaps[p].wait_recv()
        sun = jnp.maximum(join(sun_ref, 0, nodes_of[p]), 0.0)
        heats[p], ground = finish(p, other_edge[p], sun)
        return scatter(ground, nodes_of[p])

    for c in range(last // 2):
        settle(0, c)
    for c in range(last):
        settle(1, c)
    share(1)
    for c in range(last // 2, last):
        settle(0, c)
    share(0)
    table = table + shine(1)
    table = table + shine(0)
    for k in range(count):
        outbox[k] = table[k * per : (k + 1) * per]

    def send(step):
        to = lax.rem(me + step, count)
        return remote(
            outbox.at[to], inbox.at[me], flux_send.at[step], flux_recv.at[me], (to, lev)
        )

    def arrive(step):
        peer = lax.rem(me + step, count)
        return remote(
            outbox.at[peer], inbox.at[peer], flux_send.at[step], flux_recv.at[peer], (peer, lev)
        )

    def start_send(step, carry):
        send(step).start()
        return carry

    def finish_send(step, carry):
        send(step).wait_send()
        arrive(step).wait_recv()
        return carry

    lax.fori_loop(1, count, start_send, 0)
    inbox[me] = outbox[me]

    answer(last)
    part = slice(*chunks[last])
    far0[part] = far0[part] + pick(direct_buf[part], 3)
    for p in range(2):
        values = merge(p, last)
        warm = slice(2 * levels, 3 * levels)
        values = jnp.concatenate(
            [values[: 2 * levels], values[warm] + heats[p], values[3 * levels :]], axis=0
        )
        put(p, part, values)
    for copy in meta + [inner_swap] + edge_swaps:
        copy.wait_send()
    for c in range(last + 1):
        for kind in (direct, relay, cross, blend):
            kind(c).wait_send()
    lax.fori_loop(1, count, finish_send, 0)
    for k in range(count):
        table_ref[k * per : (k + 1) * per, :] = inbox[k]


def store_kernel(levels, state_ref, table_ref, index_ref, new_ref, flux_ref, sem):
    fields = state_ref.shape[0] // levels

    def store(f):
        return pltpu.make_async_copy(
            state_ref.at[f * levels : (f + 1) * levels], new_ref.at[f], sem.at[f]
        )

    for f in range(fields):
        store(f).start()
    taken = flux_ref.shape[1]
    lines = table_ref.shape[0]
    index = index_ref[...]
    here = lax.broadcasted_iota(jnp.int32, (lines, taken), 0) == index >> 7
    onehot = jnp.where(here, 1.0, 0.0).astype(BF16)
    mask = lax.broadcasted_iota(jnp.int32, (128, taken), 0) == (index & 127)
    values = table_ref[...].T
    high, _ = split2(values)
    low, tail = split2(values - high.astype(F32))
    picked = dot(high, onehot) + dot(low, onehot) + dot(tail, onehot)
    flux_ref[...] = jnp.sum(jnp.where(mask, picked, 0.0), axis=0, keepdims=True)
    for f in range(fields):
        store(f).wait()


def row_chunks(rows, skip):
    groups = (rows - skip) // 8
    edges = [skip + 8 * round(groups * share) for share in (0.0, 0.3, 0.6, 0.8, 1.0)]
    return tuple(zip(edges[:-1], edges[1:])) + ((0, skip),)


def local(
    air_state,
    metric,
    jacobian,
    edge_nbr,
    edge_side,
    coszen,
    kappa_base,
    band_kappa,
    solar_weight,
    stretch_pos,
    stretch_src,
):
    fields, levels, cols = air_state.shape
    ne = cols // NODES
    rows = fields * levels
    width = 4 * ne
    points, tracers = band_kappa.shape
    padded = -(-tracers // 8) * 8
    count = lax.axis_size("sfc")
    part = cols // lax.axis_size("lev")
    chunks = row_chunks(rows, rows - tracers * levels)
    per = max(2 * cols // count // 128, 1)
    anywhere = pl.BlockSpec(memory_space=pl.ANY)
    vmem = pl.BlockSpec(memory_space=pltpu.VMEM)
    V = pltpu.VMEM
    sems = lambda *shape: pltpu.SemaphoreType.DMA(shape)
    new, table, index = pl.pallas_call(
        functools.partial(step_kernel, count, levels, chunks),
        in_specs=[pl.BlockSpec(memory_space=pltpu.HBM)] * 11,
        out_specs=(vmem, vmem, vmem),
        out_shape=(
            pltpu.VMEM((rows, cols), F32),
            pltpu.VMEM((count * per, 128), F32),
            pltpu.VMEM((1, part), jnp.int32),
        ),
        scratch_shapes=[
            V((rows, cols), F32),
            *[V((rows, width), F32)] * 9,
            V((2, rows, width), F32),
            V((5, width, width), BF16),
            V((2, levels, points, width), F32),
            V((2, levels, width), F32),
            *[V((padded, 2 * width), F32)] * 2,
            *[V((2, padded, width), F32)] * 2,
            V((2, ne), F32),
            V((1, ne), F32),
            V((4, ne), jnp.int32),
            V((4, ne), jnp.int32),
            V((1, cols), F32),
            V((1, points), F32),
            V((tracers, points), F32),
            V((1, points), F32),
            V((1, cols), jnp.int32),
            V((1, cols), jnp.int32),
            V((4, ne), jnp.int32),
            V((4, ne), jnp.int32),
            V((1, ne), F32),
            V((1, ne), F32),
            V((8, cols), jnp.int32),
            V((count, per, 128), F32),
            V((count, per, 128), F32),
            sems(4, len(chunks)),
            sems(4, len(chunks)),
            sems(4),
            sems(4),
            sems(3),
            sems(3),
            sems(count),
            sems(count),
            sems(fields),
            sems(10),
        ],
        compiler_params=pltpu.CompilerParams(
            collective_id=0, has_side_effects=True, vmem_limit_bytes=40 * 1024 * 1024
        ),
        name="step",
    )(
        *(
            pltpu.with_memory_space_constraint(a, pltpu.HBM)
            for a in (
        air_state,
        metric,
        jacobian[None, :],
        edge_nbr,
        edge_side,
        coszen[None, :],
        kappa_base[None, :],
        band_kappa.T,
        solar_weight[None, :],
        stretch_src[None, :],
        stretch_pos[None, :],
            )
        )
    )
    new, flux = pl.pallas_call(
        functools.partial(store_kernel, levels),
        in_specs=[vmem] * 3,
        out_specs=(anywhere, vmem),
        out_shape=(
            jax.ShapeDtypeStruct(air_state.shape, F32),
            jax.ShapeDtypeStruct((1, part), F32),
        ),
        scratch_shapes=[sems(fields)],
        compiler_params=pltpu.CompilerParams(vmem_limit_bytes=8 * 1024 * 1024),
        name="store",
    )(new, table, index)
    return (new, flux.reshape(part))


def solution(mesh):
    return jax.shard_map(
        local,
        mesh=mesh,
        in_specs=(
            P(None, "lev", "sfc"),
            P(None, "sfc"),
            P("sfc"),
            P(None, "sfc"),
            P(None, "sfc"),
            P("sfc"),
            P(),
            P(),
            P(),
            P("sfc"),
            P("sfc"),
        ),
        out_specs=(P(None, "lev", "sfc"), P(("sfc", "lev"))),
        check_vma=False,
    )
```

time: 35.1 us -> 26.8 us (0.76)
  Pallas kernels: 31.5 us -> 25.9 us
  local copies, waits for them, and re-layouts: 2.69 us -> 0 us
    pallas_call x1 -> x2, Pallas kernels: 31.5 us -> 25.9 us  [the longest x1 24.3 us: local(): pl.pallas_call(functools.partial(step_kernel, count, levels, chunks), in_...]
    unnamed x4 -> x0, local copies, waits for them, and re-layouts: 2.69 us -> none
where the time goes in v1:
time: 26.8 us; the launch traced here: 26.6 us
  Pallas kernels  25.9 us (97%)
  between operations  0.64 us (2%)
    pallas_call x1, Pallas kernels, local(): pl.pallas_call(functools.partial(step_kernel, count, levels, chunks), in_...  24.3 us
    pallas_call x1, Pallas kernels, local(): pl.pallas_call(functools.partial(store_kernel, levels), in_specs=[vmem] *...  1.67 us

profile of v1, /device:TPU:0, one launch (start us, length us, event | category | flops | bytes accessed | tf_op | source)
XLA Modules:
  0.0 26.6 jit_solution(16095441955949670205)
XLA Ops:
  0.6 24.3 %step.1 = (f32[96,2048]{1,0:T(8,128)S(1)}, f32[32,128]{1,0:T(8,128)S(1)}, s32[1,1024]{1,0:T(1,128)S(1)}) custom-call(f32[24,4,2048]{2,1,0:T(4,128)} %state_ref.1, f32[2,128]{1,0:T(2,128)} %metric_hbm.1, f32[1,128]{1,0:T(1,128)} %bitcast.12, s32[4,128]{1,0:T(4,128)} %nbr_hbm.1, s32[4,128]{1,0:T(4,128)} %side_hbm.1, f32[1,2048]{1,0:T(1,128)} %bitcast.9, ...), custom_call_target="tpu_custom_call" | custom-call | tf_op jit(solution)/shard_map/step/pallas_call | solution.py:595
  24.9 1.7 %store.1 = (f32[24,4,2048]{2,1,0:T(4,128)}, f32[1,1024]{1,0:T(1,128)}) custom-call(f32[96,2048]{1,0:T(8,128)S(1)} %get-tuple-element.7.state_ref, f32[32,128]{1,0:T(8,128)S(1)} %get-tuple-element.8.table_ref, s32[1,1024]{1,0:T(1,128)S(1)} %get-tuple-element.9.index_ref), custom_call_target="tpu_custom_call" | custom-call | tf_op jit(solution)/shard_map/store/pallas_call | solution.py:663

commit v2 on v1

--- a/solution.py
+++ b/solution.py
@@ -256,8 +256,8 @@
             pl.semaphore_wait(barrier, count)
             for i in (0, 2, 3):
                 meta[i].start()
-        direct(c).start()
         if c < last:
+            direct(c).start()
             cross(c).start()
 
     def swap(part, a, b):
@@ -429,8 +429,8 @@
         answer(c)
         if 2 + c < last:
             forward(2 + c)
+    direct(last).start()
     cross(last).start()
-    forward(last)
     table = table + inner_part(1)
 
     choose(3, target, 2 - 2 * odd)
@@ -515,6 +515,7 @@
     inbox[me] = outbox[me]
 
     answer(last)
+    forward(last)
     part = slice(*chunks[last])
     far0[part] = far0[part] + pick(direct_buf[part], 3)
     for p in range(2):
@@ -534,7 +535,7 @@
         table_ref[k * per : (k + 1) * per, :] = inbox[k]
 
 
-def store_kernel(levels, state_ref, table_ref, index_ref, new_ref, flux_ref, sem):
+def store_kernel(levels, state_ref, table_ref, index_ref, new_ref, flux_out, flux_ref, sem):
     fields = state_ref.shape[0] // levels
 
     def store(f):
@@ -555,13 +556,16 @@
     low, tail = split2(values - high.astype(F32))
     picked = dot(high, onehot) + dot(low, onehot) + dot(tail, onehot)
     flux_ref[...] = jnp.sum(jnp.where(mask, picked, 0.0), axis=0, keepdims=True)
+    give = pltpu.make_async_copy(flux_ref, flux_out, sem.at[fields])
+    give.start()
     for f in range(fields):
         store(f).wait()
+    give.wait()
 
 
 def row_chunks(rows, skip):
     groups = (rows - skip) // 8
-    edges = [skip + 8 * round(groups * share) for share in (0.0, 0.3, 0.6, 0.8, 1.0)]
+    edges = [skip + 8 * round(groups * share) for share in (0.0, 0.2, 0.5, 0.8, 1.0)]
     return tuple(zip(edges[:-1], edges[1:])) + ((0, skip),)
 
 
@@ -663,12 +667,12 @@
     new, flux = pl.pallas_call(
         functools.partial(store_kernel, levels),
         in_specs=[vmem] * 3,
-        out_specs=(anywhere, vmem),
+        out_specs=(anywhere, anywhere),
         out_shape=(
             jax.ShapeDtypeStruct(air_state.shape, F32),
             jax.ShapeDtypeStruct((1, part), F32),
         ),
-        scratch_shapes=[sems(fields)],
+        scratch_shapes=[V((1, part), F32), sems(fields + 1)],
         compiler_params=pltpu.CompilerParams(vmem_limit_bytes=8 * 1024 * 1024),
         name="store",
     )(new, table, index)

time: 26.8 us -> 27.5 us (1.026)
  Pallas kernels: 25.9 us -> 26.7 us
    pallas_call x1, Pallas kernels: 24.3 us -> 25.4 us  [local(): pl.pallas_call(functools.partial(step_kernel, count, levels, chunks), in_...]
    pallas_call x1, Pallas kernels: 1.67 us -> 1.24 us  [local(): pl.pallas_call(functools.partial(store_kernel, levels), in_specs=[vmem] *...]
where the time goes in v2:
time: 27.5 us; the launch traced here: 27.3 us
  Pallas kernels  26.7 us (97%)
  between operations  0.64 us (2%)
    pallas_call x1, Pallas kernels, local(): pl.pallas_call(functools.partial(step_kernel, count, levels, chunks), in_...  25.4 us
    pallas_call x1, Pallas kernels, local(): pl.pallas_call(functools.partial(store_kernel, levels), in_specs=[vmem] *...  1.24 us

profile of v2, /device:TPU:0, one launch (start us, length us, event | category | flops | bytes accessed | tf_op | source)
XLA Modules:
  0.0 27.3 jit_solution(2437739557805863220)
XLA Ops:
  0.6 25.4 %step.1 = (f32[96,2048]{1,0:T(8,128)S(1)}, f32[32,128]{1,0:T(8,128)S(1)}, s32[1,1024]{1,0:T(1,128)S(1)}) custom-call(f32[24,4,2048]{2,1,0:T(4,128)} %state_ref.1, f32[2,128]{1,0:T(2,128)} %metric_hbm.1, f32[1,128]{1,0:T(1,128)} %bitcast.12, s32[4,128]{1,0:T(4,128)} %nbr_hbm.1, s32[4,128]{1,0:T(4,128)} %side_hbm.1, f32[1,2048]{1,0:T(1,128)} %bitcast.9, ...), custom_call_target="tpu_custom_call" | custom-call | tf_op jit(solution)/shard_map/step/pallas_call | solution.py:599
  26.1 1.2 %store.1 = (f32[24,4,2048]{2,1,0:T(4,128)}, f32[1,1024]{1,0:T(1,128)}) custom-call(f32[96,2048]{1,0:T(8,128)S(1)} %get-tuple-element.7.state_ref, f32[32,128]{1,0:T(8,128)S(1)} %get-tuple-element.8.table_ref, s32[1,1024]{1,0:T(1,128)S(1)} %get-tuple-element.9.index_ref), custom_call_target="tpu_custom_call" | custom-call | tf_op jit(solution)/shard_map/store/pallas_call | solution.py:667

commit v3 on v2

--- a/solution.py
+++ b/solution.py
@@ -256,9 +256,8 @@
             pl.semaphore_wait(barrier, count)
             for i in (0, 2, 3):
                 meta[i].start()
-        if c < last:
-            direct(c).start()
-            cross(c).start()
+        direct(c).start()
+        cross(c).start()
 
     def swap(part, a, b):
         return remote(a, b, swap_send.at[part], swap_recv.at[part], (me, 1 - lev))
@@ -429,8 +428,8 @@
         answer(c)
         if 2 + c < last:
             forward(2 + c)
-    direct(last).start()
-    cross(last).start()
+    forward(last)
+    answer(last)
     table = table + inner_part(1)
 
     choose(3, target, 2 - 2 * odd)
@@ -514,8 +513,6 @@
     lax.fori_loop(1, count, start_send, 0)
     inbox[me] = outbox[me]
 
-    answer(last)
-    forward(last)
     part = slice(*chunks[last])
     far0[part] = far0[part] + pick(direct_buf[part], 3)
     for p in range(2):

time: 27.5 us -> 26.4 us (0.960)
  Pallas kernels: 26.7 us -> 25.6 us
    pallas_call x1, Pallas kernels: 25.4 us -> 24.4 us  [local(): pl.pallas_call(functools.partial(step_kernel, count, levels, chunks), in_...]
where the time goes in v3:
time: 26.4 us; the launch traced here: 26.2 us
  Pallas kernels  25.6 us (97%)
  between operations  0.64 us (2%)
    pallas_call x1, Pallas kernels, local(): pl.pallas_call(functools.partial(step_kernel, count, levels, chunks), in_...  24.4 us
    pallas_call x1, Pallas kernels, local(): pl.pallas_call(functools.partial(store_kernel, levels), in_specs=[vmem] *...  1.24 us

profile of v3, /device:TPU:0, one launch (start us, length us, event | category | flops | bytes accessed | tf_op | source)
XLA Modules:
  0.0 26.2 jit_solution(2327761928891473469)
XLA Ops:
  0.6 24.4 %step.1 = (f32[96,2048]{1,0:T(8,128)S(1)}, f32[32,128]{1,0:T(8,128)S(1)}, s32[1,1024]{1,0:T(1,128)S(1)}) custom-call(f32[24,4,2048]{2,1,0:T(4,128)} %state_ref.1, f32[2,128]{1,0:T(2,128)} %metric_hbm.1, f32[1,128]{1,0:T(1,128)} %bitcast.12, s32[4,128]{1,0:T(4,128)} %nbr_hbm.1, s32[4,128]{1,0:T(4,128)} %side_hbm.1, f32[1,2048]{1,0:T(1,128)} %bitcast.9, ...), custom_call_target="tpu_custom_call" | custom-call | tf_op jit(solution)/shard_map/step/pallas_call | solution.py:596
  25.0 1.2 %store.1 = (f32[24,4,2048]{2,1,0:T(4,128)}, f32[1,1024]{1,0:T(1,128)}) custom-call(f32[96,2048]{1,0:T(8,128)S(1)} %get-tuple-element.7.state_ref, f32[32,128]{1,0:T(8,128)S(1)} %get-tuple-element.8.table_ref, s32[1,1024]{1,0:T(1,128)S(1)} %get-tuple-element.9.index_ref), custom_call_target="tpu_custom_call" | custom-call | tf_op jit(solution)/shard_map/store/pallas_call | solution.py:664

commit v4 on v3

--- a/solution.py
+++ b/solution.py
@@ -257,7 +257,8 @@
             for i in (0, 2, 3):
                 meta[i].start()
         direct(c).start()
-        cross(c).start()
+        if c < last:
+            cross(c).start()
 
     def swap(part, a, b):
         return remote(a, b, swap_send.at[part], swap_recv.at[part], (me, 1 - lev))
@@ -411,6 +412,7 @@
     meta[1].start()
     forward(0)
     forward(1)
+    cross(last).start()
     meta[2].wait_recv()
     meta[3].wait_recv()
     theirs = spot_of(their_nbr[...], their_side[...], partner)
@@ -476,16 +478,14 @@
         heats[p], ground = finish(p, other_edge[p], sun)
         return scatter(ground, nodes_of[p])
 
-    for c in range(last // 2):
+    for c in range(last):
         settle(0, c)
+    share(0)
     for c in range(last):
         settle(1, c)
     share(1)
-    for c in range(last // 2, last):
-        settle(0, c)
-    share(0)
+    table = table + shine(0)
     table = table + shine(1)
-    table = table + shine(0)
     for k in range(count):
         outbox[k] = table[k * per : (k + 1) * per]
 

time: 26.4 us -> 26.7 us (1.011)
  Pallas kernels: 25.6 us -> 25.9 us
    pallas_call x1, Pallas kernels: 24.4 us -> 24.6 us  [local(): pl.pallas_call(functools.partial(step_kernel, count, levels, chunks), in_...]
where the time goes in v4:
time: 26.7 us; the launch traced here: 26.5 us
  Pallas kernels  25.9 us (97%)
  between operations  0.64 us (2%)
    pallas_call x1, Pallas kernels, local(): pl.pallas_call(functools.partial(step_kernel, count, levels, chunks), in_...  24.6 us
    pallas_call x1, Pallas kernels, local(): pl.pallas_call(functools.partial(store_kernel, levels), in_specs=[vmem] *...  1.24 us

profile of v4, /device:TPU:0, one launch (start us, length us, event | category | flops | bytes accessed | tf_op | source)
XLA Modules:
  0.0 26.5 jit_solution(12989270407932799609)
XLA Ops:
  0.6 24.6 %step.1 = (f32[96,2048]{1,0:T(8,128)S(1)}, f32[32,128]{1,0:T(8,128)S(1)}, s32[1,1024]{1,0:T(1,128)S(1)}) custom-call(f32[24,4,2048]{2,1,0:T(4,128)} %state_ref.1, f32[2,128]{1,0:T(2,128)} %metric_hbm.1, f32[1,128]{1,0:T(1,128)} %bitcast.12, s32[4,128]{1,0:T(4,128)} %nbr_hbm.1, s32[4,128]{1,0:T(4,128)} %side_hbm.1, f32[1,2048]{1,0:T(1,128)} %bitcast.9, ...), custom_call_target="tpu_custom_call" | custom-call | tf_op jit(solution)/shard_map/step/pallas_call | solution.py:596
  25.3 1.2 %store.1 = (f32[24,4,2048]{2,1,0:T(4,128)}, f32[1,1024]{1,0:T(1,128)}) custom-call(f32[96,2048]{1,0:T(8,128)S(1)} %get-tuple-element.7.state_ref, f32[32,128]{1,0:T(8,128)S(1)} %get-tuple-element.8.table_ref, s32[1,1024]{1,0:T(1,128)S(1)} %get-tuple-element.9.index_ref), custom_call_target="tpu_custom_call" | custom-call | tf_op jit(solution)/shard_map/store/pallas_call | solution.py:664
